TPU v7x, 32 devices: a whole 2x2x4 slice. The times are simulated.
32 devices in a mesh: region: 4 (over y, core), block: 8 (over z, x).
Axes of the slice: x: 2, y: 2, z: 4, core: 2. Of those that a mesh axis runs over, the one named last changes fastest.
Arguments:
- features: bfloat16 [24576, 128], P(('region', 'block')), may hold values from -6 to 6
- grad_out: bfloat16 [24576, 128], P(('region', 'block')), may hold values from -6 to 6
- w1: bfloat16 [27, 128, 128], replicated, may hold values from -0.109375 to 0.109375
- w2: bfloat16 [27, 128, 128], replicated, may hold values from -0.109375 to 0.109375
- rulebook: int32 [27, 24576], P(None, ('region', 'block')), may hold values from 0 to 1024, as said below
- live_blocks: int32 [192], P(('region', 'block')), may hold values from 0 to 1, as said below
Outputs:
- grad_in: bfloat16 [24576, 128], P(('region', 'block'))
- grad_w1: float32 [27, 128, 128], replicated
- grad_w2: float32 [27, 128, 128], replicated
Inputs may be any that keep to these rules, and one draw needn't show every extreme that they name: `rulebook`: Every entry of a padded row has that value; no entry points at a padded row or at a missing neighbour; offset 27 // 2 of a live row points at the row itself. An entry of row v of slab s other than 1024 lies between v - s * 768 and v - s * 768 + 2 * 128. `live_blocks`: the first 1 and the last 1 block of every slab are live; the padded blocks of a slab lie between them. Some slab has all 6 blocks live and some slab only 2.
All inputs are finite; a program needn't handle non-finite values.
Results may differ from a plain program's by a relative error of at most 0.0039.
Values may be sent and summed in bfloat16 or wider, within the bound.
A program may use at most 64 MiB of HBM per device.

v0:
```python
import functools

import jax
import jax.numpy as jnp
from jax import lax
from jax.experimental import pallas as pl
from jax.experimental.pallas import tpu as pltpu
from jax.sharding import PartitionSpec as P

BLOCK = 128
HALO = 128
PAD = 2 * HALO
MESH = pl.DeviceIdType.MESH
F32 = jnp.float32
BF16 = jnp.bfloat16


def one_hot(matches):
    return jnp.where(matches, 1.0, 0.0).astype(BF16)


def groups_of(count):
    return 9 if count % 9 == 0 else 1


def slab_kernel(
    length,
    feat, gout, w1, w2, rule, rule_t, live,
    grad_in, partial,
    fext, aext, gpad, hpad, rpad, wc, hots, spread, spread2, picks, hidden, gext, rims, rim_in,
    send, recv,
):
    rows, chans = feat.shape
    offsets = w1.shape[0]
    blocks = rows // BLOCK
    ext_blocks = blocks + 2
    window = 3 * BLOCK
    group = groups_of(offsets)
    part_rows = partial.shape[1]
    me = lax.axis_index("block")
    left, right = me - 1, me + 1
    has_left, has_right = me > 0, me < length - 1

    def copies(i, low, low_there, high, high_there):
        down = pltpu.make_async_remote_copy(
            src_ref=low, dst_ref=low_there, send_sem=send.at[i, 0], recv_sem=recv.at[i, 0],
            device_id={"block": left}, device_id_type=MESH)
        up = pltpu.make_async_remote_copy(
            src_ref=high, dst_ref=high_there, send_sem=send.at[i, 1], recv_sem=recv.at[i, 1],
            device_id={"block": right}, device_id_type=MESH)
        return down, up

    def start(pair):
        down, up = pair
        pl.when(has_left)(down.start)
        pl.when(has_right)(up.start)

    def finish(pair):
        down, up = pair

        @pl.when(has_left)
        def _():
            down.wait_send()
            up.wait_recv()

        @pl.when(has_right)
        def _():
            up.wait_send()
            down.wait_recv()

    barrier = pltpu.get_barrier_semaphore()

    @pl.when(has_left)
    def _():
        pl.semaphore_signal(barrier, inc=1, device_id={"block": left}, device_id_type=MESH)

    @pl.when(has_right)
    def _():
        pl.semaphore_signal(barrier, inc=1, device_id={"block": right}, device_id_type=MESH)

    pl.semaphore_wait(barrier, has_left.astype(jnp.int32) + has_right.astype(jnp.int32))

    lower, upper = pl.ds(0, HALO), pl.ds(HALO + rows, HALO)
    own_low, own_high = pl.ds(HALO, HALO), pl.ds(rows, HALO)
    feat_copies = copies(0, feat.at[pl.ds(0, HALO)], fext.at[upper],
                         feat.at[pl.ds(rows - HALO, HALO)], fext.at[lower])
    act_copies = copies(1, aext.at[own_low], aext.at[upper], aext.at[own_high], aext.at[lower])
    rim_copies = [
        copies(2 + i, rims.at[i, 0], rim_in.at[i, 0], rims.at[i, 1], rim_in.at[i, 1])
        for i in range(2)
    ]
    start(feat_copies)

    edge = jnp.zeros((HALO, chans), BF16)

    @pl.when(jnp.logical_not(has_left))
    def _():
        fext[lower] = edge
        aext[lower] = edge
        for i in range(2):
            rim_in[i, 1] = edge

    @pl.when(jnp.logical_not(has_right))
    def _():
        fext[upper] = edge
        aext[upper] = edge
        for i in range(2):
            rim_in[i, 0] = edge

    fext[pl.ds(HALO, rows)] = feat[...]
    border = jnp.zeros((PAD, chans), BF16)
    for padded in (gpad, hpad):
        padded[pl.ds(0, PAD)] = border
        padded[pl.ds(PAD + rows, PAD)] = border
    gpad[pl.ds(PAD, rows)] = gout[...]
    nowhere = jnp.full((offsets, PAD), -1, jnp.int32)
    rpad[:, pl.ds(0, PAD)] = nowhere
    rpad[:, pl.ds(PAD + rows, PAD)] = nowhere
    rpad[:, pl.ds(PAD, rows)] = rule[...]

    def beside(weights):
        for k in range(offsets):
            wc[:, k * chans:(k + 1) * chans] = weights[k]

    def spread_rows(e, first, out, source):
        begin = pl.multiple_of(e * BLOCK, BLOCK)
        got = jnp.dot(hots[e, first * BLOCK:(first + group) * BLOCK, :],
                      source[pl.ds(begin, window)], preferred_element_type=F32).astype(BF16)
        for j in range(group):
            out[pl.ds(begin, BLOCK), (first + j) * chans:(first + j + 1) * chans] = (
                got[j * BLOCK:(j + 1) * BLOCK])

    def through_weights(source, i):
        @pl.loop(0, ext_blocks)
        def _(e):
            begin = pl.multiple_of(e * BLOCK, BLOCK)
            gext[pl.ds(begin, BLOCK)] = lax.dot_general(
                source[pl.ds(begin, BLOCK)], wc[...], (((1,), (1,)), ((), ())),
                preferred_element_type=F32)
        rims[i, 0] = gext[lower].astype(BF16)
        rims[i, 1] = gext[upper].astype(BF16)
        start(rim_copies[i])

    def take_rims(i):
        finish(rim_copies[i])
        gext[own_low] = gext[own_low] + rim_in[i, 1].astype(F32)
        gext[own_high] = gext[own_high] + rim_in[i, 0].astype(F32)

    def kernel_grad(extended, source, i):
        turned = extended[...].T

        @pl.loop(0, offsets // 3)
        def _(g):
            begin = pl.multiple_of(g * 3 * chans, chans)
            got = jnp.dot(turned, source[:, pl.ds(begin, 3 * chans)], preferred_element_type=F32)
            for j in range(3):
                at = pl.multiple_of((g * 3 + j) * chans, chans)
                partial[i, pl.ds(at, chans)] = got[:, j * chans:(j + 1) * chans]
        tail = part_rows - offsets * chans
        if tail:
            partial[i, pl.ds(offsets * chans, tail)] = jnp.zeros((tail, chans), F32)

    @pl.loop(0, ext_blocks)
    def _(e):
        begin = pl.multiple_of(e * BLOCK, BLOCK)
        target = lax.broadcasted_iota(jnp.int32, (BLOCK, window), 0) + e * BLOCK
        for first in range(0, offsets, group):
            for k in range(first, first + group):
                hots[e, k * BLOCK:(k + 1) * BLOCK, :] = one_hot(
                    rpad[k:k + 1, pl.ds(begin, window)] == target)
            spread_rows(e, first, spread, gpad)

    beside(w2)
    through_weights(spread, 0)

    finish(feat_copies)

    @pl.loop(0, blocks)
    def _(b):
        begin = pl.multiple_of(b * BLOCK, BLOCK)
        local = rule_t[pl.ds(begin, BLOCK)] - b * BLOCK
        columns = lax.broadcasted_iota(jnp.int32, (BLOCK, window), 1)
        framed = fext[pl.ds(begin, window)]
        for first in range(0, offsets, group):
            chosen = jnp.concatenate(
                [one_hot(local[:, k:k + 1] == columns) for k in range(first, first + group)], 0)
            got = jnp.dot(chosen, framed, preferred_element_type=F32).astype(BF16)
            for j in range(group):
                picks[:, (first + j) * chans:(first + j + 1) * chans] = (
                    got[j * BLOCK:(j + 1) * BLOCK])
        total = jnp.dot(picks[...], w1[...].reshape(offsets * chans, chans),
                        preferred_element_type=F32)
        hidden[pl.ds(begin, BLOCK)] = total
        aext[pl.ds(begin + HALO, BLOCK)] = (total / (1.0 + jnp.exp(-total))).astype(BF16)

    start(act_copies)
    take_rims(0)

    @pl.loop(0, blocks)
    def _(b):
        begin = pl.multiple_of(b * BLOCK, BLOCK)
        value = hidden[pl.ds(begin, BLOCK)]
        sigma = 1.0 / (1.0 + jnp.exp(-value))
        slope = sigma * (1.0 + value * (1.0 - sigma))
        hpad[pl.ds(begin + PAD, BLOCK)] = (gext[pl.ds(begin + HALO, BLOCK)] * slope).astype(BF16)

    @pl.loop(0, ext_blocks)
    def _(e):
        for first in range(0, offsets, group):
            spread_rows(e, first, spread2, hpad)

    beside(w1)
    through_weights(spread2, 1)
    kernel_grad(fext, spread2, 0)
    finish(act_copies)
    kernel_grad(aext, spread, 1)
    take_rims(1)
    for b in range(blocks):
        at = pl.ds(b * BLOCK, BLOCK)
        keep = live[b].astype(F32)
        grad_in[at] = (keep * (gout[at].astype(F32) + gext[pl.ds(b * BLOCK + HALO, BLOCK)])
                       ).astype(BF16)


def slab_step(features, grad_out, w1, w2, rulebook, live_blocks, part_rows):
    rows, chans = features.shape
    offsets = w1.shape[0]
    ext = rows + 2 * HALO
    blocks = rows // BLOCK
    wide = offsets * chans
    vmem = pl.BlockSpec(memory_space=pltpu.VMEM)
    return pl.pallas_call(
        functools.partial(slab_kernel, lax.axis_size("block")),
        out_shape=(
            jax.ShapeDtypeStruct((rows, chans), BF16),
            jax.ShapeDtypeStruct((2, part_rows, chans), F32),
        ),
        in_specs=[vmem] * 6 + [pl.BlockSpec(memory_space=pltpu.SMEM)],
        out_specs=(vmem, vmem),
        scratch_shapes=[
            pltpu.VMEM((ext, chans), BF16),
            pltpu.VMEM((ext, chans), BF16),
            pltpu.VMEM((rows + 2 * PAD, chans), BF16),
            pltpu.VMEM((rows + 2 * PAD, chans), BF16),
            pltpu.VMEM((offsets, rows + 2 * PAD), jnp.int32),
            pltpu.VMEM((chans, wide), BF16),
            pltpu.VMEM((blocks + 2, offsets * BLOCK, 3 * BLOCK), BF16),
            pltpu.VMEM((ext, wide), BF16),
            pltpu.VMEM((ext, wide), BF16),
            pltpu.VMEM((BLOCK, wide), BF16),
            pltpu.VMEM((rows, chans), F32),
            pltpu.VMEM((ext, chans), F32),
            pltpu.VMEM((2, 2, HALO, chans), BF16),
            pltpu.VMEM((2, 2, HALO, chans), BF16),
            pltpu.SemaphoreType.DMA((4, 2)),
            pltpu.SemaphoreType.DMA((4, 2)),
        ],
        compiler_params=pltpu.CompilerParams(
            collective_id=0, has_side_effects=True, vmem_limit_bytes=64000000),
    )(features, grad_out, w1, w2, rulebook, rulebook.T, live_blocks)


def sum_kernel(region, block, scale, part, out, own, mine, rest, got1, got2, got3,
               send, recv, send_back, recv_back):
    total = part.shape[0]
    planes, depth = region // 2 * 2, block // 2
    half = total // 2
    quarter = half // planes
    piece = quarter // depth
    r, b = lax.axis_index("region"), lax.axis_index("block")
    c, y, x, z = lax.rem(r, 2), r // 2, lax.rem(b, 2), b // 2
    p = y * 2 + x

    def device(core, plane, deep):
        return {"region": plane // 2 * 2 + core, "block": deep * 2 + lax.rem(plane, 2)}

    partner = device(1 - c, p, z)
    plane_peers = [device(c, lax.rem(p + d, planes), z) for d in range(1, planes)]
    deep_peers = [device(c, p, lax.rem(z + d, depth)) for d in range(1, depth)]
    barrier = pltpu.get_barrier_semaphore()
    for peer in [partner] + plane_peers + deep_peers:
        pl.semaphore_signal(barrier, inc=1, device_id=peer, device_id_type=MESH)
    pl.semaphore_wait(barrier, planes + depth - 1)

    def at(index, size):
        return pl.ds(pl.multiple_of(index * size, 16), size)

    def remote(src, dst, sems, i, peer):
        return pltpu.make_async_remote_copy(
            src_ref=src, dst_ref=dst, send_sem=sems[0].at[i], recv_sem=sems[1].at[i],
            device_id=peer, device_id_type=MESH)

    there = (send, recv)
    back = (send_back, recv_back)
    first = remote(part.at[at(1 - c, half)], got1, there, 0, partner)
    first.start()
    first.wait()
    mine[...] = (part[at(c, half)] + got1[...]).astype(BF16)
    second = []
    for d in range(1, planes):
        second.append(remote(mine.at[at(lax.rem(p + d, planes), quarter)], got2.at[d - 1],
                             there, d, plane_peers[d - 1]))
        second[-1].start()
    value = part[at(c * planes + p, quarter)] + got1[at(p, quarter)]
    for d in range(1, planes):
        second[d - 1].wait()
        value = value + got2[d - 1].astype(F32)
    own[...] = value
    rest[...] = value.astype(BF16)
    third = []
    for d in range(1, depth):
        third.append(remote(rest.at[at(lax.rem(z + d, depth), piece)], got3.at[d - 1],
                            there, planes - 1 + d, deep_peers[d - 1]))
        third[-1].start()
    value = own[at(z, piece)]
    for d in range(1, depth):
        third[d - 1].wait()
        value = value + got3[d - 1].astype(F32)
    place = at((c * planes + p) * depth + z, piece)
    out[place] = (value / scale).astype(BF16)
    for where, peers, base in (
        (place, deep_peers, planes),
        (at(c * planes + p, quarter), plane_peers, 1),
        (at(c, half), [partner], 0),
    ):
        moved = [remote(out.at[where], out.at[where], back, base + i, peer)
                 for i, peer in enumerate(peers)]
        for copy in moved:
            copy.start()
        for copy in moved:
            copy.wait()


def summed(part, scale):
    region, block = lax.axis_size("region"), lax.axis_size("block")
    total, chans = part.shape
    planes, depth = region // 2 * 2, block // 2
    half = total // 2
    quarter = half // planes
    piece = quarter // depth
    count = planes + depth - 1
    vmem = pl.BlockSpec(memory_space=pltpu.VMEM)
    return pl.pallas_call(
        functools.partial(sum_kernel, region, block, scale),
        out_shape=jax.ShapeDtypeStruct((total, chans), BF16),
        in_specs=[vmem],
        out_specs=vmem,
        scratch_shapes=[
            pltpu.VMEM((quarter, chans), F32),
            pltpu.VMEM((half, chans), BF16),
            pltpu.VMEM((quarter, chans), BF16),
            pltpu.VMEM((half, chans), F32),
            pltpu.VMEM((planes - 1, quarter, chans), BF16),
            pltpu.VMEM((depth - 1, piece, chans), BF16),
        ] + [pltpu.SemaphoreType.DMA((count,))] * 4,
        compiler_params=pltpu.CompilerParams(collective_id=1, has_side_effects=True),
    )(part)


def on_device(features, grad_out, w1, w2, rulebook, live_blocks):
    offsets, chans = w1.shape[0], w1.shape[1]
    devices = lax.axis_size("region") * lax.axis_size("block")
    step = 16 * devices
    part_rows = (offsets * chans + step - 1) // step * step
    grad_in, partial = slab_step(
        features, grad_out, w1, w2, rulebook, live_blocks, part_rows)
    scale = float(features.shape[0] * devices) ** 0.5
    both = summed(partial.reshape(2 * part_rows, chans), scale)
    both = both.reshape(2, part_rows, chans)[:, :offsets * chans].astype(F32)
    both = both.reshape(2, offsets, chans, chans)
    return (grad_in, both[0], both[1])


def solution(mesh):
    return jax.shard_map(
        on_device,
        mesh=mesh,
        in_specs=(
            P(("region", "block"), None),
            P(("region", "block"), None),
            P(),
            P(),
            P(None, ("region", "block")),
            P(("region", "block")),
        ),
        out_specs=(P(("region", "block"), None), P(), P()),
        check_vma=False,
    )
```

profile of v0, /device:TPU:0, one launch (start us, length us, event | category | flops | bytes accessed | tf_op | source)
XLA Modules:
  0.0 94.5 jit_solution(8147683794553436882)
XLA Ops:
  0.6 1.8 %copy.9 = s32[27,768]{0,1:T(8,128)} copy(s32[27,768]{1,0:T(8,128)} %rule.1) | data formatting | bytes 165888 | tf_op args[4]
  2.4 40.6 %shard_map.85 = (bf16[768,128]{1,0:T(8,128)(2,1)}, f32[2,3584,128]{2,1,0:T(8,128)}) custom-call(bf16[768,128]{1,0:T(8,128)(2,1)} %feat.1, bf16[768,128]{1,0:T(8,128)(2,1)} %gout.1, bf16[27,128,128]{2,1,0:T(8,128)(2,1)} %w1.1, bf16[27,128,128]{2,1,0:T(8,128)(2,1)} %w2.1, s32[27,768]{1,0:T(8,128)} %rule.1, s32[768,27]{1,0:T(8,128)} %bitcast.9, s32[6]{0:T(128)} %live.1), custom_call_target="tpu_custom_call" | custom-call | tf_op jit(solution)/shard_map/pallas_call | solution.py:232
  43.0 47.0 %shard_map.86 = bf16[7168,128]{1,0:T(8,128)(2,1)} custom-call(f32[7168,128]{1,0:T(8,128)} %bitcast.6), custom_call_target="tpu_custom_call" | custom-call | tf_op jit(solution)/shard_map/pallas_call | solution.py:343
  90.1 1.7 %slice_convert_fusion = f32[2,3456,128]{2,1,0:T(8,128)S(1)} fusion(bf16[2,3584,128]{2,1,0:T(8,128)(2,1)} %bitcast.5), kind=kLoop, calls=%fused_computation | loop fusion | flops 884736 | bytes 5308416 | tf_op jit(solution)/shard_map/convert_element_type | solution.py:369
  91.8 0.0 copy-start
  91.8 2.0 %fusion = (f32[1,3456,128]{2,1,0:T(8,128)}, f32[1,3456,128]{2,1,0:T(8,128)}) fusion(f32[2,3456,128]{2,1,0:T(8,128)S(1)} %slice_convert_fusion), kind=kLoop, calls=%fused_computation.1 | loop fusion | bytes 7077888 | tf_op jit(solution)/shard_map/slice | solution.py:371
  93.8 0.0 copy-done
  93.8 0.7 copy.11
Async XLA Ops:
  91.8 2.0 %copy-start = (bf16[768,128]{1,0:T(8,128)(2,1)S(1)}, bf16[768,128]{1,0:T(8,128)(2,1)}, u32[]{:S(2)}) copy-start(bf16[768,128]{1,0:T(8,128)(2,1)} %get-tuple-element.12) | copy-start | bytes 589828
where the time goes:
time: 95.4 us; the launch traced here: 94.5 us
  Pallas kernels  87.6 us (92%)
  local copies, waits for them, and re-layouts  4.52 us (5%)
  other arithmetic  1.71 us (2%)
    pallas_call x1, Pallas kernels, summed(): pl.pallas_call(functools.partial(sum_kernel, region, block, scale), out_s...  47 us
    pallas_call x1, Pallas kernels, slab_step(): pl.pallas_call(functools.partial(slab_kernel, lax.axis_size('block')), ou...  40.6 us
    unnamed x4, local copies, waits for them, and re-layouts  2.5 us
    slice x1, local copies, waits for them, and re-layouts, on_device(): return (grad_in, both[0], both[1])  2.02 us

commit v1 on v0

--- a/solution.py
+++ b/solution.py
@@ -24,11 +24,12 @@
 
 
 def slab_kernel(
-    length,
+    region, length, scale,
     feat, gout, w1, w2, rule, rule_t, live,
-    grad_in, partial,
+    grad_in, total_out,
     fext, aext, gpad, hpad, rpad, wc, hots, spread, spread2, picks, hidden, gext, rims, rim_in,
-    send, recv,
+    send, recv, partial, own, mine, rest, got1, got2, got3,
+    send_there, recv_there, send_back, recv_back,
 ):
     rows, chans = feat.shape
     offsets = w1.shape[0]
@@ -68,7 +69,12 @@
             up.wait_send()
             down.wait_recv()
 
+    stages, peers = sum_stages(
+        region, length, scale, partial, total_out, own, mine, rest, got1, got2, got3,
+        send_there, recv_there, send_back, recv_back)
     barrier = pltpu.get_barrier_semaphore()
+    for peer in peers:
+        pl.semaphore_signal(barrier, inc=1, device_id=peer, device_id_type=MESH)
 
     @pl.when(has_left)
     def _():
@@ -78,7 +84,8 @@
     def _():
         pl.semaphore_signal(barrier, inc=1, device_id={"block": right}, device_id_type=MESH)
 
-    pl.semaphore_wait(barrier, has_left.astype(jnp.int32) + has_right.astype(jnp.int32))
+    pl.semaphore_wait(
+        barrier, len(peers) + has_left.astype(jnp.int32) + has_right.astype(jnp.int32))
 
     lower, upper = pl.ds(0, HALO), pl.ds(HALO + rows, HALO)
     own_low, own_high = pl.ds(HALO, HALO), pl.ds(rows, HALO)
@@ -204,25 +211,42 @@
         slope = sigma * (1.0 + value * (1.0 - sigma))
         hpad[pl.ds(begin + PAD, BLOCK)] = (gext[pl.ds(begin + HALO, BLOCK)] * slope).astype(BF16)
 
+    finish(act_copies)
+    kernel_grad(aext, spread, 1)
+    ready, later = stages(1), stages(0)
+    next(ready)
+
     @pl.loop(0, ext_blocks)
     def _(e):
         for first in range(0, offsets, group):
             spread_rows(e, first, spread2, hpad)
 
+    next(ready)
+    kernel_grad(fext, spread2, 0)
+    next(later)
     beside(w1)
     through_weights(spread2, 1)
-    kernel_grad(fext, spread2, 0)
-    finish(act_copies)
-    kernel_grad(aext, spread, 1)
+    next(ready)
+    next(later)
     take_rims(1)
     for b in range(blocks):
         at = pl.ds(b * BLOCK, BLOCK)
         keep = live[b].astype(F32)
         grad_in[at] = (keep * (gout[at].astype(F32) + gext[pl.ds(b * BLOCK + HALO, BLOCK)])
                        ).astype(BF16)
-
-
-def slab_step(features, grad_out, w1, w2, rulebook, live_blocks, part_rows):
+    for _ in range(4):
+        next(ready)
+        next(later)
+    next(later, None)
+
+
+def slab_step(features, grad_out, w1, w2, rulebook, live_blocks, part_rows, scale):
+    region, block = lax.axis_size("region"), lax.axis_size("block")
+    planes, depth = region // 2 * 2, block // 2
+    half = part_rows // 2
+    quarter = half // planes
+    piece = quarter // depth
+    count = planes + depth - 1
     rows, chans = features.shape
     offsets = w1.shape[0]
     ext = rows + 2 * HALO
@@ -230,10 +254,10 @@
     wide = offsets * chans
     vmem = pl.BlockSpec(memory_space=pltpu.VMEM)
     return pl.pallas_call(
-        functools.partial(slab_kernel, lax.axis_size("block")),
+        functools.partial(slab_kernel, region, block, scale),
         out_shape=(
             jax.ShapeDtypeStruct((rows, chans), BF16),
-            jax.ShapeDtypeStruct((2, part_rows, chans), F32),
+            jax.ShapeDtypeStruct((2, part_rows, chans), BF16),
         ),
         in_specs=[vmem] * 6 + [pl.BlockSpec(memory_space=pltpu.SMEM)],
         out_specs=(vmem, vmem),
@@ -254,17 +278,23 @@
             pltpu.VMEM((2, 2, HALO, chans), BF16),
             pltpu.SemaphoreType.DMA((4, 2)),
             pltpu.SemaphoreType.DMA((4, 2)),
-        ],
+            pltpu.VMEM((2, part_rows, chans), F32),
+            pltpu.VMEM((2, quarter, chans), F32),
+            pltpu.VMEM((2, half, chans), BF16),
+            pltpu.VMEM((2, quarter, chans), BF16),
+            pltpu.VMEM((2, half, chans), F32),
+            pltpu.VMEM((2, planes - 1, quarter, chans), BF16),
+            pltpu.VMEM((2, depth - 1, piece, chans), BF16),
+        ] + [pltpu.SemaphoreType.DMA((2, count))] * 4,
         compiler_params=pltpu.CompilerParams(
             collective_id=0, has_side_effects=True, vmem_limit_bytes=64000000),
     )(features, grad_out, w1, w2, rulebook, rulebook.T, live_blocks)
 
 
-def sum_kernel(region, block, scale, part, out, own, mine, rest, got1, got2, got3,
-               send, recv, send_back, recv_back):
-    total = part.shape[0]
+def sum_stages(region, block, scale, part, out, own, mine, rest, got1, got2, got3,
+               send_there, recv_there, send_back, recv_back):
+    half = part.shape[1] // 2
     planes, depth = region // 2 * 2, block // 2
-    half = total // 2
     quarter = half // planes
     piece = quarter // depth
     r, b = lax.axis_index("region"), lax.axis_index("block")
@@ -277,84 +307,56 @@
     partner = device(1 - c, p, z)
     plane_peers = [device(c, lax.rem(p + d, planes), z) for d in range(1, planes)]
     deep_peers = [device(c, p, lax.rem(z + d, depth)) for d in range(1, depth)]
-    barrier = pltpu.get_barrier_semaphore()
-    for peer in [partner] + plane_peers + deep_peers:
-        pl.semaphore_signal(barrier, inc=1, device_id=peer, device_id_type=MESH)
-    pl.semaphore_wait(barrier, planes + depth - 1)
 
     def at(index, size):
         return pl.ds(pl.multiple_of(index * size, 16), size)
 
-    def remote(src, dst, sems, i, peer):
-        return pltpu.make_async_remote_copy(
-            src_ref=src, dst_ref=dst, send_sem=sems[0].at[i], recv_sem=sems[1].at[i],
+    def remote(src, dst, sems, i, n, peer):
+        copy = pltpu.make_async_remote_copy(
+            src_ref=src, dst_ref=dst, send_sem=sems[0].at[i, n], recv_sem=sems[1].at[i, n],
             device_id=peer, device_id_type=MESH)
-
-    there = (send, recv)
+        copy.start()
+        return copy
+
+    there = (send_there, recv_there)
     back = (send_back, recv_back)
-    first = remote(part.at[at(1 - c, half)], got1, there, 0, partner)
-    first.start()
-    first.wait()
-    mine[...] = (part[at(c, half)] + got1[...]).astype(BF16)
-    second = []
-    for d in range(1, planes):
-        second.append(remote(mine.at[at(lax.rem(p + d, planes), quarter)], got2.at[d - 1],
-                             there, d, plane_peers[d - 1]))
-        second[-1].start()
-    value = part[at(c * planes + p, quarter)] + got1[at(p, quarter)]
-    for d in range(1, planes):
-        second[d - 1].wait()
-        value = value + got2[d - 1].astype(F32)
-    own[...] = value
-    rest[...] = value.astype(BF16)
-    third = []
-    for d in range(1, depth):
-        third.append(remote(rest.at[at(lax.rem(z + d, depth), piece)], got3.at[d - 1],
-                            there, planes - 1 + d, deep_peers[d - 1]))
-        third[-1].start()
-    value = own[at(z, piece)]
-    for d in range(1, depth):
-        third[d - 1].wait()
-        value = value + got3[d - 1].astype(F32)
-    place = at((c * planes + p) * depth + z, piece)
-    out[place] = (value / scale).astype(BF16)
-    for where, peers, base in (
-        (place, deep_peers, planes),
-        (at(c * planes + p, quarter), plane_peers, 1),
-        (at(c, half), [partner], 0),
-    ):
-        moved = [remote(out.at[where], out.at[where], back, base + i, peer)
-                 for i, peer in enumerate(peers)]
-        for copy in moved:
-            copy.start()
-        for copy in moved:
-            copy.wait()
-
-
-def summed(part, scale):
-    region, block = lax.axis_size("region"), lax.axis_size("block")
-    total, chans = part.shape
-    planes, depth = region // 2 * 2, block // 2
-    half = total // 2
-    quarter = half // planes
-    piece = quarter // depth
-    count = planes + depth - 1
-    vmem = pl.BlockSpec(memory_space=pltpu.VMEM)
-    return pl.pallas_call(
-        functools.partial(sum_kernel, region, block, scale),
-        out_shape=jax.ShapeDtypeStruct((total, chans), BF16),
-        in_specs=[vmem],
-        out_specs=vmem,
-        scratch_shapes=[
-            pltpu.VMEM((quarter, chans), F32),
-            pltpu.VMEM((half, chans), BF16),
-            pltpu.VMEM((quarter, chans), BF16),
-            pltpu.VMEM((half, chans), F32),
-            pltpu.VMEM((planes - 1, quarter, chans), BF16),
-            pltpu.VMEM((depth - 1, piece, chans), BF16),
-        ] + [pltpu.SemaphoreType.DMA((count,))] * 4,
-        compiler_params=pltpu.CompilerParams(collective_id=1, has_side_effects=True),
-    )(part)
+
+    def stages(i):
+        first = remote(part.at[i, at(1 - c, half)], got1.at[i], there, i, 0, partner)
+        yield
+        first.wait()
+        mine[i] = (part[i, at(c, half)] + got1[i]).astype(BF16)
+        second = [remote(mine.at[i, at(lax.rem(p + d, planes), quarter)], got2.at[i, d - 1],
+                         there, i, d, plane_peers[d - 1]) for d in range(1, planes)]
+        yield
+        value = part[i, at(c * planes + p, quarter)] + got1[i, at(p, quarter)]
+        for d in range(1, planes):
+            second[d - 1].wait()
+            value = value + got2[i, d - 1].astype(F32)
+        own[i] = value
+        rest[i] = value.astype(BF16)
+        third = [remote(rest.at[i, at(lax.rem(z + d, depth), piece)], got3.at[i, d - 1],
+                        there, i, planes - 1 + d, deep_peers[d - 1]) for d in range(1, depth)]
+        yield
+        value = own[i, at(z, piece)]
+        for d in range(1, depth):
+            third[d - 1].wait()
+            value = value + got3[i, d - 1].astype(F32)
+        place = at((c * planes + p) * depth + z, piece)
+        out[i, place] = (value / scale).astype(BF16)
+        for where, peers, base in (
+            (place, deep_peers, planes),
+            (at(c * planes + p, quarter), plane_peers, 1),
+            (at(c, half), [partner], 0),
+        ):
+            moved = [remote(out.at[i, where], out.at[i, where], back, i, base + n, peer)
+                     for n, peer in enumerate(peers)]
+            yield
+            for copy in moved:
+                copy.wait()
+        yield
+
+    return stages, [partner] + plane_peers + deep_peers
 
 
 def on_device(features, grad_out, w1, w2, rulebook, live_blocks):
@@ -362,11 +364,10 @@
     devices = lax.axis_size("region") * lax.axis_size("block")
     step = 16 * devices
     part_rows = (offsets * chans + step - 1) // step * step
-    grad_in, partial = slab_step(
-        features, grad_out, w1, w2, rulebook, live_blocks, part_rows)
     scale = float(features.shape[0] * devices) ** 0.5
-    both = summed(partial.reshape(2 * part_rows, chans), scale)
-    both = both.reshape(2, part_rows, chans)[:, :offsets * chans].astype(F32)
+    grad_in, both = slab_step(
+        features, grad_out, w1, w2, rulebook, live_blocks, part_rows, scale)
+    both = both[:, :offsets * chans].astype(F32)
     both = both.reshape(2, offsets, chans, chans)
     return (grad_in, both[0], both[1])
 

time: 95.4 us -> 76.5 us (0.80)
  Pallas kernels: 87.6 us -> 69.5 us
    pallas_call x2 -> x1, Pallas kernels: 87.6 us -> 69.5 us  [slab_step(): pl.pallas_call(functools.partial(slab_kernel, region, block, scale), out_...]
where the time goes in v1:
time: 76.5 us; the launch traced here: 76.3 us
  Pallas kernels  69.5 us (91%)
  local copies, waits for them, and re-layouts  4.52 us (6%)
  other arithmetic  1.71 us (2%)
    pallas_call x1, Pallas kernels, slab_step(): pl.pallas_call(functools.partial(slab_kernel, region, block, scale), out_...  69.5 us
    unnamed x4, local copies, waits for them, and re-layouts  2.5 us
    slice x1, local copies, waits for them, and re-layouts, on_device(): return (grad_in, both[0], both[1])  2.02 us
    convert_element_type x1, other arithmetic, on_device(): both = both[:, :offsets * chans].astype(F32)  1.71 us

profile of v1, /device:TPU:0, one launch (start us, length us, event | category | flops | bytes accessed | tf_op | source)
XLA Modules:
  0.0 76.3 jit_solution(6144138338748647990)
XLA Ops:
  0.6 1.8 %copy.9 = s32[27,768]{0,1:T(8,128)} copy(s32[27,768]{1,0:T(8,128)} %rule.1) | data formatting | bytes 165888 | tf_op args[4]
  2.4 69.5 %shard_map.85 = (bf16[768,128]{1,0:T(8,128)(2,1)}, bf16[2,3584,128]{2,1,0:T(8,128)(2,1)}) custom-call(bf16[768,128]{1,0:T(8,128)(2,1)} %feat.1, bf16[768,128]{1,0:T(8,128)(2,1)} %gout.1, bf16[27,128,128]{2,1,0:T(8,128)(2,1)} %w1.1, bf16[27,128,128]{2,1,0:T(8,128)(2,1)} %w2.1, s32[27,768]{1,0:T(8,128)} %rule.1, s32[768,27]{1,0:T(8,128)} %bitcast.5, s32[6]{0:T(128)} %live.1), custom_call_target="tpu_custom_call" | custom-call | tf_op jit(solution)/shard_map/pallas_call | solution.py:256
  71.9 1.7 %slice_convert_fusion = f32[2,3456,128]{2,1,0:T(8,128)S(1)} fusion(bf16[2,3584,128]{2,1,0:T(8,128)(2,1)} %get-tuple-element.6), kind=kLoop, calls=%fused_computation | loop fusion | flops 884736 | bytes 5308416 | tf_op jit(solution)/shard_map/convert_element_type | solution.py:370
  73.6 0.0 copy-start
  73.6 2.0 %fusion = (f32[1,3456,128]{2,1,0:T(8,128)}, f32[1,3456,128]{2,1,0:T(8,128)}) fusion(f32[2,3456,128]{2,1,0:T(8,128)S(1)} %slice_convert_fusion), kind=kLoop, calls=%fused_computation.1 | loop fusion | bytes 7077888 | tf_op jit(solution)/shard_map/slice | solution.py:372
  75.7 0.0 copy-done
  75.7 0.7 copy.11
Async XLA Ops:
  73.6 2.0 %copy-start = (bf16[768,128]{1,0:T(8,128)(2,1)S(1)}, bf16[768,128]{1,0:T(8,128)(2,1)}, u32[]{:S(2)}) copy-start(bf16[768,128]{1,0:T(8,128)(2,1)} %get-tuple-element.12) | copy-start | bytes 589828

commit v2 on v1

--- a/solution.py
+++ b/solution.py
@@ -24,12 +24,11 @@
 
 
 def slab_kernel(
-    region, length, scale,
+    region, length, scale, parts,
     feat, gout, w1, w2, rule, rule_t, live,
     grad_in, total_out,
     fext, aext, gpad, hpad, rpad, wc, hots, spread, spread2, picks, hidden, gext, rims, rim_in,
-    send, recv, partial, own, mine, rest, got1, got2, got3,
-    send_there, recv_there, send_back, recv_back,
+    send, recv, partial, send_there, recv_there, send_back, recv_back, *held
 ):
     rows, chans = feat.shape
     offsets = w1.shape[0]
@@ -37,7 +36,6 @@
     ext_blocks = blocks + 2
     window = 3 * BLOCK
     group = groups_of(offsets)
-    part_rows = partial.shape[1]
     me = lax.axis_index("block")
     left, right = me - 1, me + 1
     has_left, has_right = me > 0, me < length - 1
@@ -70,7 +68,7 @@
             down.wait_recv()
 
     stages, peers = sum_stages(
-        region, length, scale, partial, total_out, own, mine, rest, got1, got2, got3,
+        region, length, scale, parts, partial, total_out, held,
         send_there, recv_there, send_back, recv_back)
     barrier = pltpu.get_barrier_semaphore()
     for peer in peers:
@@ -129,7 +127,7 @@
         for k in range(offsets):
             wc[:, k * chans:(k + 1) * chans] = weights[k]
 
-    def spread_rows(e, first, out, source):
+    def spread_rows(e, first, group, out, source):
         begin = pl.multiple_of(e * BLOCK, BLOCK)
         got = jnp.dot(hots[e, first * BLOCK:(first + group) * BLOCK, :],
                       source[pl.ds(begin, window)], preferred_element_type=F32).astype(BF16)
@@ -155,17 +153,21 @@
 
     def kernel_grad(extended, source, i):
         turned = extended[...].T
-
-        @pl.loop(0, offsets // 3)
+        first, last, base, size = parts[i]
+        count = last - first
+        unit = next(u for u in (4, 3, 2, 1) if count % u == 0)
+
+        @pl.loop(0, count // unit)
         def _(g):
-            begin = pl.multiple_of(g * 3 * chans, chans)
-            got = jnp.dot(turned, source[:, pl.ds(begin, 3 * chans)], preferred_element_type=F32)
-            for j in range(3):
-                at = pl.multiple_of((g * 3 + j) * chans, chans)
-                partial[i, pl.ds(at, chans)] = got[:, j * chans:(j + 1) * chans]
-        tail = part_rows - offsets * chans
+            begin = pl.multiple_of((first + g * unit) * chans, chans)
+            got = jnp.dot(turned, source[:, pl.ds(begin, unit * chans)],
+                          preferred_element_type=F32)
+            for j in range(unit):
+                at = pl.multiple_of(base + (g * unit + j) * chans, chans)
+                partial[pl.ds(at, chans)] = got[:, j * chans:(j + 1) * chans]
+        tail = size - count * chans
         if tail:
-            partial[i, pl.ds(offsets * chans, tail)] = jnp.zeros((tail, chans), F32)
+            partial[pl.ds(base + count * chans, tail)] = jnp.zeros((tail, chans), F32)
 
     @pl.loop(0, ext_blocks)
     def _(e):
@@ -175,7 +177,7 @@
             for k in range(first, first + group):
                 hots[e, k * BLOCK:(k + 1) * BLOCK, :] = one_hot(
                     rpad[k:k + 1, pl.ds(begin, window)] == target)
-            spread_rows(e, first, spread, gpad)
+            spread_rows(e, first, group, spread, gpad)
 
     beside(w2)
     through_weights(spread, 0)
@@ -212,21 +214,33 @@
         hpad[pl.ds(begin + PAD, BLOCK)] = (gext[pl.ds(begin + HALO, BLOCK)] * slope).astype(BF16)
 
     finish(act_copies)
-    kernel_grad(aext, spread, 1)
-    ready, later = stages(1), stages(0)
+    kernel_grad(aext, spread, 2)
+    ready, middle, later = stages(2), stages(0), stages(1)
     next(ready)
+    cut = parts[0][1]
+    portion = 8 if cut % 8 == 0 else cut
 
     @pl.loop(0, ext_blocks)
     def _(e):
-        for first in range(0, offsets, group):
-            spread_rows(e, first, spread2, hpad)
+        for first in range(0, cut, portion):
+            spread_rows(e, first, portion, spread2, hpad)
 
     next(ready)
     kernel_grad(fext, spread2, 0)
+    next(middle)
+
+    @pl.loop(0, ext_blocks)
+    def _(e):
+        spread_rows(e, cut, offsets - cut, spread2, hpad)
+
+    next(ready)
+    next(middle)
+    kernel_grad(fext, spread2, 1)
     next(later)
     beside(w1)
     through_weights(spread2, 1)
     next(ready)
+    next(middle)
     next(later)
     take_rims(1)
     for b in range(blocks):
@@ -234,19 +248,30 @@
         keep = live[b].astype(F32)
         grad_in[at] = (keep * (gout[at].astype(F32) + gext[pl.ds(b * BLOCK + HALO, BLOCK)])
                        ).astype(BF16)
-    for _ in range(4):
-        next(ready)
-        next(later)
-    next(later, None)
-
-
-def slab_step(features, grad_out, w1, w2, rulebook, live_blocks, part_rows, scale):
+    for _ in range(5):
+        next(ready, None)
+        next(middle, None)
+        next(later, None)
+
+
+def slab_step(features, grad_out, w1, w2, rulebook, live_blocks, parts, scale):
     region, block = lax.axis_size("region"), lax.axis_size("block")
     planes, depth = region // 2 * 2, block // 2
-    half = part_rows // 2
-    quarter = half // planes
-    piece = quarter // depth
     count = planes + depth - 1
+    total = sum(part[3] for part in parts)
+
+    def held_of(size):
+        half = size // 2
+        quarter = half // planes
+        return [
+            pltpu.VMEM((quarter, chans), F32),
+            pltpu.VMEM((half, chans), BF16),
+            pltpu.VMEM((quarter, chans), BF16),
+            pltpu.VMEM((half, chans), F32),
+            pltpu.VMEM((planes - 1, quarter, chans), BF16),
+            pltpu.VMEM((depth - 1, quarter // depth, chans), BF16),
+        ]
+
     rows, chans = features.shape
     offsets = w1.shape[0]
     ext = rows + 2 * HALO
@@ -254,10 +279,10 @@
     wide = offsets * chans
     vmem = pl.BlockSpec(memory_space=pltpu.VMEM)
     return pl.pallas_call(
-        functools.partial(slab_kernel, region, block, scale),
+        functools.partial(slab_kernel, region, block, scale, parts),
         out_shape=(
             jax.ShapeDtypeStruct((rows, chans), BF16),
-            jax.ShapeDtypeStruct((2, part_rows, chans), BF16),
+            jax.ShapeDtypeStruct((total, chans), BF16),
         ),
         in_specs=[vmem] * 6 + [pl.BlockSpec(memory_space=pltpu.SMEM)],
         out_specs=(vmem, vmem),
@@ -278,25 +303,17 @@
             pltpu.VMEM((2, 2, HALO, chans), BF16),
             pltpu.SemaphoreType.DMA((4, 2)),
             pltpu.SemaphoreType.DMA((4, 2)),
-            pltpu.VMEM((2, part_rows, chans), F32),
-            pltpu.VMEM((2, quarter, chans), F32),
-            pltpu.VMEM((2, half, chans), BF16),
-            pltpu.VMEM((2, quarter, chans), BF16),
-            pltpu.VMEM((2, half, chans), F32),
-            pltpu.VMEM((2, planes - 1, quarter, chans), BF16),
-            pltpu.VMEM((2, depth - 1, piece, chans), BF16),
-        ] + [pltpu.SemaphoreType.DMA((2, count))] * 4,
+            pltpu.VMEM((total, chans), F32),
+        ] + [pltpu.SemaphoreType.DMA((len(parts), count))] * 4 + [
+            one for part in parts for one in held_of(part[3])],
         compiler_params=pltpu.CompilerParams(
             collective_id=0, has_side_effects=True, vmem_limit_bytes=64000000),
     )(features, grad_out, w1, w2, rulebook, rulebook.T, live_blocks)
 
 
-def sum_stages(region, block, scale, part, out, own, mine, rest, got1, got2, got3,
+def sum_stages(region, block, scale, parts, partial, total_out, held,
                send_there, recv_there, send_back, recv_back):
-    half = part.shape[1] // 2
     planes, depth = region // 2 * 2, block // 2
-    quarter = half // planes
-    piece = quarter // depth
     r, b = lax.axis_index("region"), lax.axis_index("block")
     c, y, x, z = lax.rem(r, 2), r // 2, lax.rem(b, 2), b // 2
     p = y * 2 + x
@@ -322,34 +339,40 @@
     back = (send_back, recv_back)
 
     def stages(i):
-        first = remote(part.at[i, at(1 - c, half)], got1.at[i], there, i, 0, partner)
+        base, size = parts[i][2:]
+        part, out = partial.at[pl.ds(base, size)], total_out.at[pl.ds(base, size)]
+        own, mine, rest, got1, got2, got3 = held[6 * i:6 * i + 6]
+        half = size // 2
+        quarter = half // planes
+        piece = quarter // depth
+        first = remote(part.at[at(1 - c, half)], got1, there, i, 0, partner)
         yield
         first.wait()
-        mine[i] = (part[i, at(c, half)] + got1[i]).astype(BF16)
-        second = [remote(mine.at[i, at(lax.rem(p + d, planes), quarter)], got2.at[i, d - 1],
+        mine[...] = (part[at(c, half)] + got1[...]).astype(BF16)
+        second = [remote(mine.at[at(lax.rem(p + d, planes), quarter)], got2.at[d - 1],
                          there, i, d, plane_peers[d - 1]) for d in range(1, planes)]
         yield
-        value = part[i, at(c * planes + p, quarter)] + got1[i, at(p, quarter)]
+        value = part[at(c * planes + p, quarter)] + got1[at(p, quarter)]
         for d in range(1, planes):
             second[d - 1].wait()
-            value = value + got2[i, d - 1].astype(F32)
-        own[i] = value
-        rest[i] = value.astype(BF16)
-        third = [remote(rest.at[i, at(lax.rem(z + d, depth), piece)], got3.at[i, d - 1],
+            value = value + got2[d - 1].astype(F32)
+        own[...] = value
+        rest[...] = value.astype(BF16)
+        third = [remote(rest.at[at(lax.rem(z + d, depth), piece)], got3.at[d - 1],
                         there, i, planes - 1 + d, deep_peers[d - 1]) for d in range(1, depth)]
         yield
-        value = own[i, at(z, piece)]
+        value = own[at(z, piece)]
         for d in range(1, depth):
             third[d - 1].wait()
-            value = value + got3[i, d - 1].astype(F32)
+            value = value + got3[d - 1].astype(F32)
         place = at((c * planes + p) * depth + z, piece)
-        out[i, place] = (value / scale).astype(BF16)
+        out[place] = (value / scale).astype(BF16)
         for where, peers, base in (
             (place, deep_peers, planes),
             (at(c * planes + p, quarter), plane_peers, 1),
             (at(c, half), [partner], 0),
         ):
-            moved = [remote(out.at[i, where], out.at[i, where], back, i, base + n, peer)
+            moved = [remote(out.at[where], out.at[where], back, i, base + n, peer)
                      for n, peer in enumerate(peers)]
             yield
             for copy in moved:
@@ -363,13 +386,19 @@
     offsets, chans = w1.shape[0], w1.shape[1]
     devices = lax.axis_size("region") * lax.axis_size("block")
     step = 16 * devices
-    part_rows = (offsets * chans + step - 1) // step * step
+    cut = offsets * 3 // 5
+    parts, base = [], 0
+    for first, last in ((0, cut), (cut, offsets), (0, offsets)):
+        size = ((last - first) * chans + step - 1) // step * step
+        parts.append((first, last, base, size))
+        base += size
     scale = float(features.shape[0] * devices) ** 0.5
     grad_in, both = slab_step(
-        features, grad_out, w1, w2, rulebook, live_blocks, part_rows, scale)
-    both = both[:, :offsets * chans].astype(F32)
-    both = both.reshape(2, offsets, chans, chans)
-    return (grad_in, both[0], both[1])
+        features, grad_out, w1, w2, rulebook, live_blocks, tuple(parts), scale)
+    low, high, second = [
+        both[base:base + (last - first) * chans].astype(F32) for first, last, base, _ in parts]
+    first = jnp.concatenate([low, high], 0)
+    return (grad_in, first.reshape(w1.shape), second.reshape(w1.shape))
 
 
 def solution(mesh):

time: 76.5 us -> 78.6 us (1.027)
  Pallas kernels: 69.5 us -> 70.9 us
  other arithmetic: 1.71 us -> 2.81 us
    reshape x0 -> x2, other arithmetic: none -> 2.81 us  [on_device(): return (grad_in, first.reshape(w1.shape), second.reshape(w1.shape))]
    convert_element_type x1 -> x0, other arithmetic: 1.71 us -> none  [on_device(): both = both[:, :offsets * chans].astype(F32)]
    pallas_call x1, Pallas kernels: 69.5 us -> 70.9 us  [slab_step(): pl.pallas_call(functools.partial(slab_kernel, region, block, scale, parts...]
where the time goes in v2:
time: 78.6 us; the launch traced here: 78.4 us
  Pallas kernels  70.9 us (90%)
  local copies, waits for them, and re-layouts  4.05 us (5%)
  other arithmetic  2.81 us (4%)
    pallas_call x1, Pallas kernels, slab_step(): pl.pallas_call(functools.partial(slab_kernel, region, block, scale, parts...  70.9 us
    reshape x2, other arithmetic, on_device(): return (grad_in, first.reshape(w1.shape), second.reshape(w1.shape))  2.81 us
    unnamed x4, local copies, waits for them, and re-layouts  2.5 us

profile of v2, /device:TPU:0, one launch (start us, length us, event | category | flops | bytes accessed | tf_op | source)
XLA Modules:
  0.0 78.4 jit_solution(17290676091730761635)
XLA Ops:
  0.6 1.8 %copy.9 = s32[27,768]{0,1:T(8,128)} copy(s32[27,768]{1,0:T(8,128)} %rule.1) | data formatting | bytes 165888 | tf_op args[4]
  2.4 70.9 %shard_map.85 = (bf16[768,128]{1,0:T(8,128)(2,1)}, bf16[7168,128]{1,0:T(8,128)(2,1)}) custom-call(bf16[768,128]{1,0:T(8,128)(2,1)} %feat.1, bf16[768,128]{1,0:T(8,128)(2,1)} %gout.1, bf16[27,128,128]{2,1,0:T(8,128)(2,1)} %w1.1, bf16[27,128,128]{2,1,0:T(8,128)(2,1)} %w2.1, s32[27,768]{1,0:T(8,128)} %rule.1, s32[768,27]{1,0:T(8,128)} %bitcast.7, s32[6]{0:T(128)} %live.1), custom_call_target="tpu_custom_call" | custom-call | tf_op jit(solution)/shard_map/pallas_call | solution.py:281
  73.3 1.6 %fusion = (bf16[3456,128]{1,0:T(8,128)(2,1)S(1)}, bf16[3456,128]{1,0:T(8,128)(2,1)S(1)}) fusion(bf16[7168,128]{1,0:T(8,128)(2,1)} %get-tuple-element.6), kind=kLoop, calls=%fused_computation | loop fusion | bytes 3538944 | tf_op jit(solution)/shard_map/slice | solution.py:399
  74.9 1.4 %convert.3 = f32[27,128,128]{2,1,0:T(8,128)} convert(bf16[27,128,128]{2,1,0:T(8,128)(2,1)S(1)} %bitcast.6) | non-fusion elementwise | flops 442368 | bytes 2654208 | tf_op jit(solution)/shard_map/reshape | solution.py:401
  76.3 0.0 copy-start
  76.3 1.4 %convert.4 = f32[27,128,128]{2,1,0:T(8,128)} convert(bf16[27,128,128]{2,1,0:T(8,128)(2,1)S(1)} %bitcast.5) | non-fusion elementwise | flops 442368 | bytes 2654208 | tf_op jit(solution)/shard_map/reshape | solution.py:401
  77.7 0.0 copy-done
  77.7 0.7 copy.11
Async XLA Ops:
  76.3 1.4 %copy-start = (bf16[768,128]{1,0:T(8,128)(2,1)S(1)}, bf16[768,128]{1,0:T(8,128)(2,1)}, u32[]{:S(2)}) copy-start(bf16[768,128]{1,0:T(8,128)(2,1)} %get-tuple-element.12) | copy-start | bytes 589828

commit v3 on v1

--- a/solution.py
+++ b/solution.py
@@ -216,28 +216,31 @@
     ready, later = stages(1), stages(0)
     next(ready)
 
-    @pl.loop(0, ext_blocks)
-    def _(e):
-        for first in range(0, offsets, group):
-            spread_rows(e, first, spread2, hpad)
-
+    def spread_blocks(begin, end):
+        @pl.loop(begin, end)
+        def _(e):
+            for first in range(0, offsets, group):
+                spread_rows(e, first, spread2, hpad)
+
+    spread_blocks(0, ext_blocks // 2)
     next(ready)
+    spread_blocks(ext_blocks // 2, ext_blocks)
     kernel_grad(fext, spread2, 0)
     next(later)
+    next(ready)
     beside(w1)
     through_weights(spread2, 1)
+    next(later)
     next(ready)
-    next(later)
     take_rims(1)
     for b in range(blocks):
         at = pl.ds(b * BLOCK, BLOCK)
         keep = live[b].astype(F32)
         grad_in[at] = (keep * (gout[at].astype(F32) + gext[pl.ds(b * BLOCK + HALO, BLOCK)])
                        ).astype(BF16)
-    for _ in range(4):
-        next(ready)
-        next(later)
-    next(later, None)
+    for _ in range(5):
+        next(ready, None)
+        next(later, None)
 
 
 def slab_step(features, grad_out, w1, w2, rulebook, live_blocks, part_rows, scale):

time: 76.5 us -> 77.6 us (1.014)
  Pallas kernels: 69.5 us -> 70.5 us
    pallas_call x1, Pallas kernels: 69.5 us -> 70.5 us  [slab_step(): pl.pallas_call(functools.partial(slab_kernel, region, block, scale), out_...]
where the time goes in v3:
time: 77.6 us; the launch traced here: 77.4 us
  Pallas kernels  70.5 us (91%)
  local copies, waits for them, and re-layouts  4.52 us (6%)
  other arithmetic  1.71 us (2%)
    pallas_call x1, Pallas kernels, slab_step(): pl.pallas_call(functools.partial(slab_kernel, region, block, scale), out_...  70.5 us
    unnamed x4, local copies, waits for them, and re-layouts  2.5 us
    slice x1, local copies, waits for them, and re-layouts, on_device(): return (grad_in, both[0], both[1])  2.02 us
    convert_element_type x1, other arithmetic, on_device(): both = both[:, :offsets * chans].astype(F32)  1.71 us

profile of v3, /device:TPU:0, one launch (start us, length us, event | category | flops | bytes accessed | tf_op | source)
XLA Modules:
  0.0 77.4 jit_solution(7672791054720631562)
XLA Ops:
  0.6 1.8 %copy.9 = s32[27,768]{0,1:T(8,128)} copy(s32[27,768]{1,0:T(8,128)} %rule.1) | data formatting | bytes 165888 | tf_op args[4]
  2.4 70.5 %shard_map.85 = (bf16[768,128]{1,0:T(8,128)(2,1)}, bf16[2,3584,128]{2,1,0:T(8,128)(2,1)}) custom-call(bf16[768,128]{1,0:T(8,128)(2,1)} %feat.1, bf16[768,128]{1,0:T(8,128)(2,1)} %gout.1, bf16[27,128,128]{2,1,0:T(8,128)(2,1)} %w1.1, bf16[27,128,128]{2,1,0:T(8,128)(2,1)} %w2.1, s32[27,768]{1,0:T(8,128)} %rule.1, s32[768,27]{1,0:T(8,128)} %bitcast.5, s32[6]{0:T(128)} %live.1), custom_call_target="tpu_custom_call" | custom-call | tf_op jit(solution)/shard_map/pallas_call | solution.py:259
  73.0 1.7 %slice_convert_fusion = f32[2,3456,128]{2,1,0:T(8,128)S(1)} fusion(bf16[2,3584,128]{2,1,0:T(8,128)(2,1)} %get-tuple-element.6), kind=kLoop, calls=%fused_computation | loop fusion | flops 884736 | bytes 5308416 | tf_op jit(solution)/shard_map/convert_element_type | solution.py:373
  74.7 0.0 copy-start
  74.7 2.0 %fusion = (f32[1,3456,128]{2,1,0:T(8,128)}, f32[1,3456,128]{2,1,0:T(8,128)}) fusion(f32[2,3456,128]{2,1,0:T(8,128)S(1)} %slice_convert_fusion), kind=kLoop, calls=%fused_computation.1 | loop fusion | bytes 7077888 | tf_op jit(solution)/shard_map/slice | solution.py:375
  76.7 0.0 copy-done
  76.7 0.7 copy.11
Async XLA Ops:
  74.7 2.0 %copy-start = (bf16[768,128]{1,0:T(8,128)(2,1)S(1)}, bf16[768,128]{1,0:T(8,128)(2,1)}, u32[]{:S(2)}) copy-start(bf16[768,128]{1,0:T(8,128)(2,1)} %get-tuple-element.12) | copy-start | bytes 589828
